TPU v7x, 256 devices: a whole 4x4x8 slice. The times are simulated.
256 devices in a mesh: frame: 8 (over z), tile: 32 (over x, y, core).
Axes of the slice: x: 4, y: 4, z: 8, core: 2. Of those that a mesh axis runs over, the one named last changes fastest.
Arguments:
- displacement: bfloat16 [512, 2, 32, 4096], P('frame', None, 'tile'), may hold values from -256 to 256
Outputs:
- basis: bfloat16 [512, 3, 32, 4096], P(None, None, 'tile', 'frame')
- factor: float32 [512, 512], replicated
All inputs are finite; a program needn't handle non-finite values.
Results may differ from a plain program's by a relative error of at most 0.0053.
The roundings to bfloat16 on the way count: a program that leaves them out, or rounds other values in their place, can miss the bound.
Values may be sent and summed in bfloat16 or wider, within the bound.
No kernel may reach another device: no remote copies, remote signals or barrier semaphores. Data moves between devices by JAX's collectives and lax.ppermute only.
A program may use at most 64 MiB of HBM per device.

v0:
```python
import math
import jax
import jax.numpy as jnp
from jax import lax
from jax.sharding import PartitionSpec as P


def with_halo(array, sides, width):
    for axis, dim in sides:
        peers, length = (lax.axis_size(axis), array.shape[dim])
        up = [(i, (i + 1) % peers) for i in range(peers - 1)]
        down = [(j, i) for i, j in up]
        last = lax.slice_in_dim(array, length - width, length, axis=dim)
        first = lax.slice_in_dim(array, 0, width, axis=dim)
        before = lax.ppermute(last, axis, up)
        after = lax.ppermute(first, axis, down)
        array = jnp.concatenate([before, array, after], axis=dim)
    return array


def derivative(center, before, after, first, final):
    return jnp.where(
        first, after - center, jnp.where(final, center - before, (after - before) * 0.5)
    )


def column_derivative(center):
    width = center.shape[-1]
    after = jnp.concatenate([center[..., 1:], center[..., -1:]], axis=-1)
    before = jnp.concatenate([center[..., :1], center[..., :-1]], axis=-1)
    column = jnp.arange(width, dtype=jnp.int32)
    return derivative(center, before, after, column == 0, column == width - 1)


def combine_strain(d_rows, d_cols):
    return jnp.stack(
        [d_cols[:, 0], d_rows[:, 1], 0.5 * (d_rows[:, 0] + d_cols[:, 1])], axis=1
    ).astype(jnp.bfloat16)


def local(displacement):
    rows = displacement.shape[2]
    full_width = displacement.shape[3]
    total_rows = lax.axis_size("tile") * rows
    scale = math.sqrt(3 * total_rows * full_width)
    row_global = lax.axis_index("tile") * rows + jnp.arange(rows, dtype=jnp.int32)
    first = (row_global == 0)[:, None]
    final = (row_global == total_rows - 1)[:, None]
    padded = with_halo(displacement, (("tile", 2),), 1)
    field = padded.astype(jnp.float32)
    center = field[:, :, 1:-1, :]
    d_rows = derivative(center, field[:, :, :-2, :], field[:, :, 2:, :], first, final)
    d_cols = column_derivative(center)
    strain = combine_strain(d_rows, d_cols)
    pixel_major = lax.all_to_all(strain, "frame", split_axis=3, concat_axis=0, tiled=True)
    frames = pixel_major.shape[0]
    snapshot_half = pixel_major.reshape(frames, -1)
    local_gram = lax.dot_general(
        snapshot_half, snapshot_half, (((1,), (1,)), ((), ())), preferred_element_type=jnp.float32
    )
    gram = lax.psum(local_gram, ("frame", "tile"))
    lower = jnp.linalg.cholesky(gram)
    snapshot = snapshot_half.astype(jnp.float32)
    solved = lax.linalg.triangular_solve(lower, snapshot, left_side=True, lower=True)
    basis = (solved * scale).astype(jnp.bfloat16).reshape(pixel_major.shape)
    return (basis, lower.T / scale)


def solution(mesh):
    return jax.shard_map(
        local,
        mesh=mesh,
        in_specs=(P("frame", None, "tile", None),),
        out_specs=(P(None, None, "tile", "frame"), P()),
        check_vma=False,
    )
```

profile of v0, /device:TPU:2, one launch (start us, length us, event | category | flops | bytes accessed | tf_op | source)
XLA Modules:
  0.0 526.9 jit_solution(18431249091505621572)
XLA Ops:
  9.0 1.9 collective-permute-start
  10.9 5.8 %collective-permute-start.1 = (bf16[64,2,1,4096]{3,0,2,1:T(8,128)(2,1)S(1)}, bf16[64,2,1,4096]{3,0,2,1:T(8,128)(2,1)S(1)}, u32[]{:S(2)}, u32[]{:S(2)}) collective-permute-start(bf16[64,2,1,4096]{3,0,2,1:T(8,128)(2,1)S(1)} %copy.46), channel_id=1, source_target_pairs={{1,0},{2,1},{3,2},{4,3},{5,4},{6,5},{7,6},{8,7},{9,8},{10,9},{11,1... | collective-permute-start | bytes 3145736 | tf_op jit(solution)/shard_map/ppermute | solution.py:16
  16.7 10.5 %collective-permute-done = bf16[64,2,1,4096]{3,0,2,1:T(8,128)(2,1)S(1)} collective-permute-done((bf16[64,2,1,4096]{3,0,2,1:T(8,128)(2,1)S(1)}, bf16[64,2,1,4096]{3,0,2,1:T(8,128)(2,1)S(1)}, u32[]{:S(2)}, u32[]{:S(2)}) %collective-permute-start) | collective-permute-done | bytes 1048608 | tf_op jit(solution)/shard_map/ppermute | solution.py:15
  32.2 4.7 copy.49
  36.9 6.1 %reshape.243 = bf16[8,2,49152]{2,1,0:T(2,128)(2,1)S(1)} reshape(bf16[4096,1,3,64]{3,2,1,0:T(4,128)(2,1)} %bitcast.77) | data formatting | bytes 3145728
  43.0 48.1 %all_to_all.15 = bf16[8,2,49152]{2,1,0:T(2,128)(2,1)S(1)} all-to-all(bf16[8,2,49152]{2,1,0:T(2,128)(2,1)S(1)} %reshape.243), channel_id=1, replica_groups=mesh['frame'=8,'tile'=32] {'frame'}, dimensions={0} | all-to-all | bytes 3145728 | tf_op jit(solution)/shard_map/all_to_all | solution.py:55
  91.2 4.8 reshape.244
  96.0 4.8 copy.67
  102.7 2.0 fusion.36
  104.9 2.1 convert_element_type.26
  108.2 248.2 %all-reduce.3.cloned.1.call-done = f32[512,512]{0,1:T(8,128)} async-done(((f32[512,512]{0,1:T(8,128)}), f32[512,512]{0,1:T(8,128)}) %all-reduce.3.cloned.1.call-update) | async-done | bytes 1048592 | tf_op jit(solution)/shard_map/psum | solution.py:61
  358.3 11.7 %cholesky.104 = f32[128,128]{1,0:T(8,128)S(1)} custom-call(f32[128,128]{1,0:T(8,128)S(1)} %cholesky.266), custom_call_target="Cholesky" | custom-call | tf_op jit(solution)/shard_map/jit(cholesky)/cholesky | solution.py:62
  370.2 9.8 %custom-call.30 = f32[1,128,128]{1,2,0:T(8,128)S(1)} custom-call(f32[1,128,128]{2,1,0:T(8,128)S(1)} %get-tuple-element.45), custom_call_target="InvertDiagBlocksLowerTriangular" | custom-call | tf_op jit(solution)/shard_map/jit(cholesky)/cholesky | solution.py:62
  380.7 11.8 %cholesky.217 = f32[128,128]{1,0:T(8,128)S(1)} custom-call(f32[128,128]{1,0:T(8,128)S(1)} %cholesky.270), custom_call_target="Cholesky" | custom-call | tf_op jit(solution)/shard_map/jit(cholesky)/cholesky | solution.py:62
  393.8 9.8 %custom-call.31 = f32[1,128,128]{1,2,0:T(8,128)S(1)} custom-call(f32[1,128,128]{2,1,0:T(8,128)S(1)} %get-tuple-element.42), custom_call_target="InvertDiagBlocksLowerTriangular" | custom-call | tf_op jit(solution)/shard_map/jit(cholesky)/cholesky | solution.py:62
  404.3 11.7 %cholesky.238 = f32[128,128]{1,0:T(8,128)S(1)} custom-call(f32[128,128]{1,0:T(8,128)S(1)} %cholesky.275), custom_call_target="Cholesky" | custom-call | tf_op jit(solution)/shard_map/jit(cholesky)/cholesky | solution.py:62
  416.7 9.8 %custom-call.32 = f32[1,128,128]{1,2,0:T(8,128)S(1)} custom-call(f32[1,128,128]{2,1,0:T(8,128)S(1)} %get-tuple-element.39), custom_call_target="InvertDiagBlocksLowerTriangular" | custom-call | tf_op jit(solution)/shard_map/jit(cholesky)/cholesky | solution.py:62
  427.1 11.9 %cholesky.255 = f32[128,128]{1,0:T(8,128)S(1)} custom-call(f32[128,128]{1,0:T(8,128)S(1)} %convolution_subtract_fusion.5), custom_call_target="Cholesky" | custom-call | tf_op jit(solution)/shard_map/jit(cholesky)/cholesky | solution.py:62
  442.6 10.0 %while.1 = (s32[]{:T(128)}, f32[512,512]{1,0:T(8,128)S(1)}, s32[4,2]{0,1:T(2,128)S(1)}, f32[4,128,128]{2,1,0:T(8,128)}, s32[]{:T(128)}) while((s32[]{:T(128)}, f32[512,512]{1,0:T(8,128)S(1)}, s32[4,2]{0,1:T(2,128)S(1)}, f32[4,128,128]{2,1,0:T(8,128)}, s32[]{:T(128)}) %tuple.39), condition=%wide.while_cond, body=%wide.while_body.sunk | while | flops 2 | bytes 132705 | solution.py:64
  452.6 40.2 %custom-call.33 = f32[4,128,128]{1,2,0:T(8,128)S(1)} custom-call(f32[4,128,128]{2,1,0:T(8,128)} %get-tuple-element.9), custom_call_target="InvertDiagBlocksLowerTriangular" | custom-call | tf_op jit(solution)/shard_map/triangular_solve | solution.py:64
  494.4 2.1 convolution_subtract_fusion.2
  501.9 3.4 fusion.1
  513.5 2.3 copy.60
  517.1 2.7 fusion.7
  (76 shorter events, 43.4 us)
Async XLA Ops:
  7.2 349.3 %all-reduce.3.cloned.1.call-start = ((), (), s32[]{:S(2)}) async-start(), calls=%async_computation.1 | async-start | bytes 2097152 | tf_op jit(solution)/shard_map/psum | solution.py:61
  9.0 18.2 %collective-permute-start = (bf16[64,2,1,4096]{3,0,2,1:T(8,128)(2,1)S(1)}, bf16[64,2,1,4096]{3,0,2,1:T(8,128)(2,1)S(1)}, u32[]{:S(2)}, u32[]{:S(2)}) collective-permute-start(bf16[64,2,1,4096]{3,0,2,1:T(8,128)(2,1)S(1)} %copy.46), channel_id=1, source_target_pairs={{0,1},{1,2},{2,3},{3,4},{4,5},{5,6},{6,7},{7,8},{8,9},{9,10},{10,1... | collective-permute-start | bytes 3145736 | tf_op jit(solution)/shard_map/ppermute | solution.py:15
  10.9 18.1 %collective-permute-start.1 = (bf16[64,2,1,4096]{3,0,2,1:T(8,128)(2,1)S(1)}, bf16[64,2,1,4096]{3,0,2,1:T(8,128)(2,1)S(1)}, u32[]{:S(2)}, u32[]{:S(2)}) collective-permute-start(bf16[64,2,1,4096]{3,0,2,1:T(8,128)(2,1)S(1)} %copy.46), channel_id=1, source_target_pairs={{1,0},{2,1},{3,2},{4,3},{5,4},{6,5},{7,6},{8,7},{9,8},{10,9},{11,1... | collective-permute-start | bytes 3145736 | tf_op jit(solution)/shard_map/ppermute | solution.py:16
  356.4 1.7 copy-start.1
  452.6 40.2 %copy-start.3 = (f32[512,512]{1,0:T(8,128)}, f32[512,512]{1,0:T(8,128)S(1)}, u32[]{:S(2)}) copy-start(f32[512,512]{1,0:T(8,128)S(1)} %get-tuple-element.100) | copy-start | bytes 3145732
  492.8 1.6 copy-start.4
  494.4 3.8 copy-start
  507.6 4.3 copy-start.2
Sparse Core Ops, SparseCore 0:
  104.8 251.5 all-reduce.2
where the time goes:
time: 532 us; the launch traced here: 527 us
  waiting for transfers between devices  261 us (49%)
  other arithmetic  127 us (24%)
  local copies, waits for them, and re-layouts  48.3 us (9%)
  blocking collectives  48.1 us (9%)
  matrix products  17.9 us (3%)
  between operations  17.2 us (3%)
  starting transfers between devices  7.71 us (1%)
    psum x1, waiting for transfers between devices, local(): gram = lax.psum(local_gram, ('frame', 'tile'))  248 us
    another operation x15, other arithmetic, local(): lower = jnp.linalg.cholesky(gram)  79.4 us
    all_to_all x1, blocking collectives, local(): lax.all_to_all(strain, 'frame', split_axis=3, concat_axis=0, tiled=True)  48.1 us
    another operation x2, other arithmetic, local(): lax.linalg.triangular_solve(lower, snapshot, left_side=True, lower=True)  40.2 us
    unnamed x16, local copies, waits for them, and re-layouts  15.4 us
    another operation x7, matrix products, local(): lax.linalg.triangular_solve(lower, snapshot, left_side=True, lower=True)  14.1 us
  transfers between devices with their start and end apart: 3, of which 3 were waited for; matrix products, arithmetic and copies ran while one was open for 1% of the time, Pallas kernels for 0%

commit v1 on v0

--- a/solution.py
+++ b/solution.py
@@ -58,7 +58,7 @@
     local_gram = lax.dot_general(
         snapshot_half, snapshot_half, (((1,), (1,)), ((), ())), preferred_element_type=jnp.float32
     )
-    gram = lax.psum(local_gram, ("frame", "tile"))
+    gram = lax.psum(lax.psum(local_gram, "tile"), "frame")
     lower = jnp.linalg.cholesky(gram)
     snapshot = snapshot_half.astype(jnp.float32)
     solved = lax.linalg.triangular_solve(lower, snapshot, left_side=True, lower=True)

time: 532 us -> 471 us (0.89)
  waiting for transfers between devices: 261 us -> 197 us
    psum x1 -> x2, waiting for transfers between devices: 248 us -> 185 us  [local(): gram = lax.psum(lax.psum(local_gram, 'tile'), 'frame')]
  transfers between devices with their start and end apart: 3 -> 4, of which waited for: 3 -> 4; matrix products, arithmetic and copies ran while one was open for 1% -> 1% of each run, Pallas kernels for 0% -> 0%
where the time goes in v1:
time: 471 us; the launch traced here: 464 us
  waiting for transfers between devices  197 us (42%)
  other arithmetic  127 us (27%)
  blocking collectives  48.1 us (10%)
  local copies, waits for them, and re-layouts  47.8 us (10%)
  matrix products  17.9 us (4%)
  between operations  17.2 us (4%)
  starting transfers between devices  8.22 us (2%)
    psum x2, waiting for transfers between devices, local(): gram = lax.psum(lax.psum(local_gram, 'tile'), 'frame')  185 us
    another operation x15, other arithmetic, local(): lower = jnp.linalg.cholesky(gram)  79.4 us
    all_to_all x1, blocking collectives, local(): lax.all_to_all(strain, 'frame', split_axis=3, concat_axis=0, tiled=True)  48.1 us
    another operation x2, other arithmetic, local(): lax.linalg.triangular_solve(lower, snapshot, left_side=True, lower=True)  40.2 us
    unnamed x16, local copies, waits for them, and re-layouts  15.4 us
    another operation x7, matrix products, local(): lax.linalg.triangular_solve(lower, snapshot, left_side=True, lower=True)  14.1 us
    ppermute x1, waiting for transfers between devices, with_halo(): before = lax.ppermute(last, axis, up)  10.5 us
    another operation x12, local copies, waits for them, and re-layouts  9.98 us
  transfers between devices with their start and end apart: 4, of which 4 were waited for; matrix products, arithmetic and copies ran while one was open for 1% of the time, Pallas kernels for 0%

profile of v1, /device:TPU:2, one launch (start us, length us, event | category | flops | bytes accessed | tf_op | source)
XLA Modules:
  0.0 463.6 jit_solution(6460907395932185622)
XLA Ops:
  10.9 5.8 %collective-permute-start.1 = (bf16[64,2,1,4096]{3,0,2,1:T(8,128)(2,1)S(1)}, bf16[64,2,1,4096]{3,0,2,1:T(8,128)(2,1)S(1)}, u32[]{:S(2)}, u32[]{:S(2)}) collective-permute-start(bf16[64,2,1,4096]{3,0,2,1:T(8,128)(2,1)S(1)} %copy.46), channel_id=1, source_target_pairs={{1,0},{2,1},{3,2},{4,3},{5,4},{6,5},{7,6},{8,7},{9,8},{10,9},{11,1... | collective-permute-start | bytes 3145736 | tf_op jit(solution)/shard_map/ppermute | solution.py:16
  16.7 10.5 %collective-permute-done = bf16[64,2,1,4096]{3,0,2,1:T(8,128)(2,1)S(1)} collective-permute-done((bf16[64,2,1,4096]{3,0,2,1:T(8,128)(2,1)S(1)}, bf16[64,2,1,4096]{3,0,2,1:T(8,128)(2,1)S(1)}, u32[]{:S(2)}, u32[]{:S(2)}) %collective-permute-start) | collective-permute-done | bytes 1048608 | tf_op jit(solution)/shard_map/ppermute | solution.py:15
  32.2 4.7 %copy.49 = bf16[64,3,1,4096]{0,1,2,3:T(4,128)(2,1)} copy(bf16[64,3,1,4096]{3,0,2,1:T(8,128)(2,1)S(1)} %pad_maximum_fusion.2) | data formatting | bytes 3145728 | tf_op jit(solution)/shard_map/stack | solution.py:36
  36.9 6.1 %reshape.243 = bf16[8,2,49152]{2,1,0:T(2,128)(2,1)S(1)} reshape(bf16[4096,1,3,64]{3,2,1,0:T(4,128)(2,1)} %bitcast.77) | data formatting | bytes 3145728
  43.0 48.1 %all_to_all.15 = bf16[8,2,49152]{2,1,0:T(2,128)(2,1)S(1)} all-to-all(bf16[8,2,49152]{2,1,0:T(2,128)(2,1)S(1)} %reshape.243), channel_id=1, replica_groups=mesh['frame'=8,'tile'=32] {'frame'}, dimensions={0} | all-to-all | bytes 3145728 | tf_op jit(solution)/shard_map/all_to_all | solution.py:55
  91.2 4.8 %reshape.244 = bf16[4096,1,3,64]{3,2,1,0:T(4,128)(2,1)} reshape(bf16[8,2,49152]{2,1,0:T(2,128)(2,1)S(1)} %all_to_all.15) | data formatting | bytes 3145728
  96.0 4.3 copy.67
  102.2 2.0 fusion.36
  104.7 109.7 %all-reduce.4.cloned.1.call-done = f32[512,512]{0,1:T(8,128)} async-done(((f32[512,512]{0,1:T(8,128)}), f32[512,512]{0,1:T(8,128)}) %all-reduce.4.cloned.1.call-update) | async-done | bytes 1048592 | tf_op jit(solution)/shard_map/psum | solution.py:61
  214.7 2.1 convert_element_type.26
  218.0 75.2 %all-reduce.6.cloned.1.call-done = f32[512,512]{0,1:T(8,128)} async-done(((f32[512,512]{0,1:T(8,128)}), f32[512,512]{0,1:T(8,128)}) %all-reduce.6.cloned.1.call-update) | async-done | bytes 1048592 | tf_op jit(solution)/shard_map/psum | solution.py:61
  295.1 11.7 %cholesky.104 = f32[128,128]{1,0:T(8,128)S(1)} custom-call(f32[128,128]{1,0:T(8,128)S(1)} %cholesky.266), custom_call_target="Cholesky" | custom-call | tf_op jit(solution)/shard_map/jit(cholesky)/cholesky | solution.py:62
  307.0 9.8 %custom-call.30 = f32[1,128,128]{1,2,0:T(8,128)S(1)} custom-call(f32[1,128,128]{2,1,0:T(8,128)S(1)} %get-tuple-element.45), custom_call_target="InvertDiagBlocksLowerTriangular" | custom-call | tf_op jit(solution)/shard_map/jit(cholesky)/cholesky | solution.py:62
  317.5 11.7 %cholesky.217 = f32[128,128]{1,0:T(8,128)S(1)} custom-call(f32[128,128]{1,0:T(8,128)S(1)} %cholesky.270), custom_call_target="Cholesky" | custom-call | tf_op jit(solution)/shard_map/jit(cholesky)/cholesky | solution.py:62
  330.4 10.0 %custom-call.31 = f32[1,128,128]{1,2,0:T(8,128)S(1)} custom-call(f32[1,128,128]{2,1,0:T(8,128)S(1)} %get-tuple-element.42), custom_call_target="InvertDiagBlocksLowerTriangular" | custom-call | tf_op jit(solution)/shard_map/jit(cholesky)/cholesky | solution.py:62
  341.1 11.7 %cholesky.238 = f32[128,128]{1,0:T(8,128)S(1)} custom-call(f32[128,128]{1,0:T(8,128)S(1)} %cholesky.275), custom_call_target="Cholesky" | custom-call | tf_op jit(solution)/shard_map/jit(cholesky)/cholesky | solution.py:62
  353.5 9.8 %custom-call.32 = f32[1,128,128]{1,2,0:T(8,128)S(1)} custom-call(f32[1,128,128]{2,1,0:T(8,128)S(1)} %get-tuple-element.39), custom_call_target="InvertDiagBlocksLowerTriangular" | custom-call | tf_op jit(solution)/shard_map/jit(cholesky)/cholesky | solution.py:62
  363.9 11.9 %cholesky.255 = f32[128,128]{1,0:T(8,128)S(1)} custom-call(f32[128,128]{1,0:T(8,128)S(1)} %convolution_subtract_fusion.5), custom_call_target="Cholesky" | custom-call | tf_op jit(solution)/shard_map/jit(cholesky)/cholesky | solution.py:62
  379.3 10.0 %while.1 = (s32[]{:T(128)}, f32[512,512]{1,0:T(8,128)S(1)}, s32[4,2]{0,1:T(2,128)S(1)}, f32[4,128,128]{2,1,0:T(8,128)}, s32[]{:T(128)}) while((s32[]{:T(128)}, f32[512,512]{1,0:T(8,128)S(1)}, s32[4,2]{0,1:T(2,128)S(1)}, f32[4,128,128]{2,1,0:T(8,128)}, s32[]{:T(128)}) %tuple.39), condition=%wide.while_cond, body=%wide.while_body.sunk | while | flops 2 | bytes 132705 | solution.py:64
  389.3 40.2 %custom-call.33 = f32[4,128,128]{1,2,0:T(8,128)S(1)} custom-call(f32[4,128,128]{2,1,0:T(8,128)} %get-tuple-element.9), custom_call_target="InvertDiagBlocksLowerTriangular" | custom-call | tf_op jit(solution)/shard_map/triangular_solve | solution.py:64
  431.2 2.1 convolution_subtract_fusion.2
  438.6 3.4 fusion.1
  450.2 2.3 copy.60
  453.9 2.7 fusion.7
  (79 shorter events, 45.8 us)
Async XLA Ops:
  7.2 207.3 %all-reduce.4.cloned.1.call-start = ((), (), s32[]{:S(2)}) async-start(), calls=%async_computation.1 | async-start | bytes 2097152 | tf_op jit(solution)/shard_map/psum | solution.py:61
  9.0 18.2 %collective-permute-start = (bf16[64,2,1,4096]{3,0,2,1:T(8,128)(2,1)S(1)}, bf16[64,2,1,4096]{3,0,2,1:T(8,128)(2,1)S(1)}, u32[]{:S(2)}, u32[]{:S(2)}) collective-permute-start(bf16[64,2,1,4096]{3,0,2,1:T(8,128)(2,1)S(1)} %copy.46), channel_id=1, source_target_pairs={{0,1},{1,2},{2,3},{3,4},{4,5},{5,6},{6,7},{7,8},{8,9},{9,10},{10,1... | collective-permute-start | bytes 3145736 | tf_op jit(solution)/shard_map/ppermute | solution.py:15
  10.9 18.1 %collective-permute-start.1 = (bf16[64,2,1,4096]{3,0,2,1:T(8,128)(2,1)S(1)}, bf16[64,2,1,4096]{3,0,2,1:T(8,128)(2,1)S(1)}, u32[]{:S(2)}, u32[]{:S(2)}) collective-permute-start(bf16[64,2,1,4096]{3,0,2,1:T(8,128)(2,1)S(1)} %copy.46), channel_id=1, source_target_pairs={{1,0},{2,1},{3,2},{4,3},{5,4},{6,5},{7,6},{8,7},{9,8},{10,9},{11,1... | collective-permute-start | bytes 3145736 | tf_op jit(solution)/shard_map/ppermute | solution.py:16
  104.2 189.0 %all-reduce.6.cloned.1.call-start = ((), (), s32[]{:S(2)}) async-start(), calls=%async_computation.2 | async-start | bytes 2097152 | tf_op jit(solution)/shard_map/psum | solution.py:61
  293.2 1.7 copy-start.1
  389.3 40.2 %copy-start.3 = (f32[512,512]{1,0:T(8,128)}, f32[512,512]{1,0:T(8,128)S(1)}, u32[]{:S(2)}) copy-start(f32[512,512]{1,0:T(8,128)S(1)} %get-tuple-element.101) | copy-start | bytes 3145732
  429.5 1.6 copy-start.4
  431.2 3.8 copy-start
  444.3 4.3 copy-start.2
Sparse Core Ops, SparseCore 0:
  104.3 110.0 all-reduce.3
  216.9 76.2 all-reduce.5
